TPU v7x, 32 devices: a whole 2x2x4 slice. The times are simulated.
32 devices in a mesh: row: 4 (over y, x), col: 8 (over z, core).
Axes of the slice: x: 2, y: 2, z: 4, core: 2. Of those that a mesh axis runs over, the one named last changes fastest.
Arguments:
- trail: float32 [2, 4, 512, 2, 8, 512], P(None, 'row', None, None, 'col'), may hold values from -6 to 6
- panel: float32 [2, 4, 512, 512], P(None, 'row', None, 'col'), may hold values from -6 to 6
- row_basis: float32 [2, 4, 64, 512], P(None, 'row', None, 'col'), may hold values from -0.75 to 0.75
- row_coeff: float32 [2, 4, 64, 512], P(None, 'row', None, 'col'), may hold values from -0.25 to 0.25
- col_basis: float32 [2, 8, 64, 512], P(None, 'col', None, 'row'), may hold values from -0.75 to 0.75
- col_scaled: float32 [2, 8, 64, 512], P(None, 'col', None, 'row'), may hold values from -0.25 to 0.25
- pivot_basis: float32 [64, 512], P(None, 'col'), may hold values from -0.75 to 0.75
- pivot_scaled: float32 [64, 512], replicated, may hold values from -0.25 to 0.25
- sketch: float32 [64, 512], replicated, may hold values from -6 to 6
- perm: int32 [512], replicated, may hold values from 0 to 511, each once
- pair_kind: int32 [256], replicated, may hold values from 0 to 1
- pivot_values: float32 [3, 256], replicated, may hold values from -3 to 3, as said below
Outputs:
- trail_out: float32 [2, 4, 512, 2, 8, 512], P(None, 'row', None, None, 'col')
- basis_out: float32 [2, 4, 64, 512], P(None, 'row')
- coeff_out: float32 [2, 4, 64, 512], P(None, 'row')
Inputs may be any that keep to these rules, and one draw needn't show every extreme that they name: `pivot_values`: rows 0 and 1 have magnitudes between 0.5 and 0.7; row 2 has magnitude 1.2 or more.
All inputs are finite; a program needn't handle non-finite values.
Results may differ from a plain program's by a relative error of at most 0.00013.
Values sent between devices are 32-bit elements; how exact they have to be, the bound alone decides.
No kernel may reach another device: no remote copies, remote signals or barrier semaphores. Data moves between devices by JAX's collectives and lax.ppermute only.
A program may use at most 64 MiB of HBM per device.

v0:
```python
import jax
import jax.numpy as jnp
from jax import lax
from jax.sharding import PartitionSpec as P


def pair_apply(rows, pair_kind, pivot_values):
    shaped = rows.reshape(rows.shape[:-1] + (rows.shape[-1] // 2, 2))
    first_in = shaped[..., 0]
    second_in = shaped[..., 1]
    diag_one = pivot_values[0]
    diag_two = pivot_values[1]
    offdiag = pivot_values[2]
    determinant = diag_one * diag_two - offdiag * offdiag
    twin = pair_kind == 1
    first = jnp.where(
        twin, (first_in * diag_two - second_in * offdiag) / determinant, first_in / diag_one
    )
    second = jnp.where(
        twin, (second_in * diag_one - first_in * offdiag) / determinant, second_in / diag_two
    )
    return jnp.stack([first, second], axis=-1).reshape(rows.shape)


def tri_solve(lower, rhs):
    return jax.vmap(lambda low, right: jax.scipy.linalg.solve_triangular(low, right, lower=True))(
        lower, rhs
    )


def body(
    trail,
    panel,
    row_basis,
    row_coeff,
    col_basis,
    col_scaled,
    pivot_basis,
    pivot_scaled,
    sketch,
    perm,
    pair_kind,
    pivot_values,
):
    highest = lax.Precision.HIGHEST
    width = sketch.shape[1]
    block = panel.shape[3]
    xrows, yrows = (
        lax.all_gather(row_basis, "col", axis=3, tiled=True),
        lax.all_gather(row_coeff, "col", axis=3, tiled=True),
    )
    zcols, gcols = (
        lax.all_gather(col_basis, "row", axis=3, tiled=True),
        lax.all_gather(col_scaled, "row", axis=3, tiled=True),
    )
    xrows = xrows[:, 0]
    yrows = yrows[:, 0]
    zcols = zcols[:, 0]
    gcols = gcols[:, 0]
    core = jnp.einsum("arp,bsp->arbs", yrows, gcols, precision=highest)
    left = jnp.einsum("arp,arbs->apbs", xrows, core, precision=highest)
    change = jnp.einsum("apbs,bsq->apbq", left, zcols, precision=highest)
    trail_out = trail - change[:, None, :, :, None, :]
    pcore = jnp.einsum("arp,sp->ars", yrows, pivot_scaled, precision=highest)
    pleft = jnp.einsum("arp,ars->aps", xrows, pcore, precision=highest)
    updated = panel[:, 0] - jnp.einsum("aps,sq->apq", pleft, pivot_basis, precision=highest)
    scaled_t = pair_apply(sketch, pair_kind, pivot_values)
    column_ids = lax.axis_index("col") * block + jnp.arange(block, dtype=jnp.int32)
    selector = (perm[:, None] == column_ids[None, :]).astype(jnp.float32)
    local_sketch = jnp.dot(scaled_t, selector, precision=highest)
    partial_range = jnp.einsum("apq,rq->arp", updated, local_sketch, precision=highest)
    range_t = lax.psum(partial_range, "col")
    gram = jnp.einsum("arp,asp->ars", range_t, range_t, precision=highest) / width
    basis = tri_solve(jnp.linalg.cholesky(gram), range_t)
    projected_part = jnp.einsum("arp,apq->arq", basis, updated, precision=highest)
    projected = lax.all_gather(projected_part, "col", axis=2, tiled=True)
    permuted = jnp.take(projected, perm, axis=2)
    coeff = pair_apply(permuted, pair_kind, pivot_values) / jnp.sqrt(jnp.float32(width))
    return (trail_out, basis[:, None], coeff[:, None])


def solution(mesh):
    return jax.shard_map(
        body,
        mesh=mesh,
        in_specs=(
            P(None, "row", None, None, "col", None),
            P(None, "row", None, "col"),
            P(None, "row", None, "col"),
            P(None, "row", None, "col"),
            P(None, "col", None, "row"),
            P(None, "col", None, "row"),
            P(None, "col"),
            P(),
            P(),
            P(),
            P(),
            P(),
        ),
        out_specs=(
            P(None, "row", None, None, "col", None),
            P(None, "row", None, None),
            P(None, "row", None, None),
        ),
        check_vma=False,
    )
```

profile of v0, /device:TPU:0, one launch (start us, length us, event | category | flops | bytes accessed | tf_op | source)
XLA Modules:
  0.0 159.1 jit_solution(12313392400558865005)
XLA Ops:
  7.2 0.0 copy-start
  7.2 0.0 copy-start.6
  7.2 0.0 all-reduce.2.cloned.1.call-start
  7.3 0.8 broadcast_compare_fusion
  8.1 0.8 fusion.16
  8.9 0.9 copy.54
  9.8 0.9 copy.51
  10.8 1.0 copy.59
  11.8 16.5 %all_gather.15 = f32[2,1,64,512]{2,0,1,3:T(2,128)S(1)} all-gather(f32[2,1,64,64]{2,0,1,3:T(2,128)S(1)} %copy.51), channel_id=1, replica_groups=mesh['row'=4,'col'=8] {'col'}, dimensions={3}, use_global_device_ids=true | all-gather | bytes 294912 | tf_op jit(solution)/shard_map/all_gather | solution.py:50
  28.3 0.2 copy.52
  28.5 14.8 %all_gather.17 = f32[2,1,64,512]{2,0,1,3:T(2,128)S(1)} all-gather(f32[2,1,64,64]{2,0,1,3:T(2,128)S(1)} %copy.54), channel_id=1, replica_groups=mesh['row'=4,'col'=8] {'col'}, dimensions={3}, use_global_device_ids=true | all-gather | bytes 294912 | tf_op jit(solution)/shard_map/all_gather | solution.py:49
  43.3 0.2 copy.55
  43.5 2.2 %broadcast_select_fusion.4 = (f32[64,256,1]{0,2,1:T(1,128)S(1)}, f32[64,256,1]{0,2,1:T(1,128)S(1)}) fusion(pred[256]{0:T(512)(128)(4,1)S(1)} %broadcast_compare_fusion, f32[64,256,2]{0,2,1:T(2,128)S(1)} %bitcast.82, f32[256]{0:T(256)S(1)} %bitcast.90, f32[256]{0:T(256)S(1)} %bitcast.96, f32[256]{0:T(256)S(1)} %bitcast.93, f32[256]{0:T(256)S(1)} %bitcast.87), kind=kLoop, calls=%fused_computation.21 | loop fusion | flops 196608 | bytes 266496 | tf_op jit(solution)/shard_map/jit(_where)/select_n | solution.py:16
  45.7 0.3 pad_maximum_fusion
  46.0 0.5 fusion.6
  46.5 0.4 convolution_bitcast_fusion.2
  46.8 0.0 copy-done.6
  46.8 0.5 convolution_bitcast_fusion.3
  47.3 0.0 copy-done.5
  47.3 0.0 copy-done.2
  47.3 0.4 convolution_subtract_fusion
  47.7 1.1 convolution_bitcast_fusion.1
  48.8 0.0 all-reduce.2.cloned.1.call-update
  48.9 10.3 %all_gather.18 = f32[2,1,64,512]{3,2,0,1:T(8,128)S(1)} all-gather(f32[2,1,64,128]{3,2,0,1:T(8,128)S(1)} %bitcast.85), channel_id=1, replica_groups=mesh['row'=4,'col'=8] {'row'}, dimensions={3}, use_global_device_ids=true | all-gather | bytes 327680 | tf_op jit(solution)/shard_map/all_gather | solution.py:53
  59.2 10.2 %all_gather.16 = f32[2,1,64,512]{3,2,0,1:T(8,128)S(1)} all-gather(f32[2,1,64,128]{3,2,0,1:T(8,128)S(1)} %bitcast.86), channel_id=1, replica_groups=mesh['row'=4,'col'=8] {'row'}, dimensions={3}, use_global_device_ids=true | all-gather | bytes 327680 | tf_op jit(solution)/shard_map/all_gather | solution.py:54
  69.4 0.5 fusion.1
  69.9 0.6 convolution_bitcast_fusion
  70.5 7.2 %bitcast_subtract_fusion = f32[2,1,512,2,1,512]{5,2,0,3,4,1:T(8,128)} fusion(f32[2,1,512,2,1,512]{5,4,3,2,1,0:T(1,128)} %param.12, f32[2,512,2,64]{1,3,0,2:T(8,128)S(1)} %convolution_bitcast_fusion, f32[2,1,64,512]{3,2,0,1:T(8,128)S(1)} %all_gather.18), kind=kOutput, calls=%fused_computation.1 | convolution fusion | flops 806354944 | bytes 9175040 | tf_op jit(solution)/shard_map/apbs,bsq->apbq/dot_general | solution.py:62
  77.7 0.2 broadcast_in_dim.45
  77.9 8.5 %copy.66 = f32[2,1,512,2,1,512]{5,4,3,2,1,0:T(1,128)} copy(f32[2,1,512,2,1,512]{5,2,0,3,4,1:T(8,128)} %bitcast_subtract_fusion) | data formatting | bytes 8388608
  86.4 19.4 %all-reduce.2.cloned.1.call-done = f32[2,64,512]{2,1,0:T(8,128)} async-done(((f32[2,64,512]{2,1,0:T(8,128)}), f32[2,64,512]{2,1,0:T(8,128)}) %all-reduce.2.cloned.1.call-update) | async-done | bytes 262160 | tf_op jit(solution)/shard_map/psum | solution.py:72
  105.8 1.4 fusion.17
  107.2 0.1 copy.62
  107.3 11.7 %custom-call.8 = f32[2,64,64]{2,1,0:T(8,128)S(1)} custom-call(f32[2,64,64]{2,1,0:T(8,128)S(1)} %fusion.14), custom_call_target="Cholesky" | custom-call | tf_op jit(solution)/shard_map/jit(cholesky)/cholesky | solution.py:74
  119.1 0.1 compare_reduce_fusion
  119.2 0.1 select_bitcast_fusion
  119.3 9.8 %custom-call.9 = f32[2,1,64,64]{2,3,1,0:T(8,128)S(1)} custom-call(f32[2,1,64,64]{3,2,1,0:T(8,128)S(1)} %select_bitcast_fusion), custom_call_target="InvertDiagBlocksLowerTriangular" | custom-call | tf_op jit(solution)/shard_map/vmap(jit(_solve_triangular))/triangular_solve | solution.py:26
  129.1 1.4 fusion.12
  130.5 0.0 copy-start.1
  130.5 0.4 fusion.18
  130.9 0.1 copy.64
  131.0 15.1 %all_gather.19 = f32[2,64,512]{1,0,2:T(2,128)S(1)} all-gather(f32[2,64,64]{1,0,2:T(2,128)S(1)} %copy.64), channel_id=1, replica_groups=mesh['row'=4,'col'=8] {'col'}, dimensions={2}, use_global_device_ids=true | all-gather | bytes 294912 | tf_op jit(solution)/shard_map/all_gather | solution.py:76
  146.1 2.1 %gather_fusion = f32[512,2,64]{2,1,0:T(2,128)S(1)} fusion(f32[2,64,512]{1,0,2:T(2,128)S(1)} %all_gather.19, s32[1024]{0:T(1024)S(1)} %pad_clamp_fusion), kind=kCustom, calls=%fused_computation | custom fusion | bytes 526336 | tf_op jit(solution)/shard_map/jit(_take)/gather | solution.py:77
  148.2 0.4 broadcast_select_fusion.2
  148.6 2.2 %broadcast_select_fusion.1 = (f32[2,64,256,1]{1,3,2,0:T(1,128)S(1)}, f32[2,64,256,1]{1,3,2,0:T(1,128)S(1)}) fusion(pred[256]{0:T(512)(128)(4,1)S(1)} %broadcast_compare_fusion, f32[2,64,256,2]{1,3,2,0:T(2,128)S(1)} %broadcast_select_fusion.2, f32[256]{0:T(256)S(1)} %bitcast.92, f32[256]{0:T(256)S(1)} %multiply_subtract_fusion, f32[256]{0:T(256)S(1)} %bitcast.95, ...), kind=kLoop, calls=%fused_computation.9 | loop fusion | flops 393216 | bytes 528640 | tf_op jit(solution)/shard_map/jit(_where)/select_n | solution.py:16
  150.8 0.6 maximum_multiply_fusion
  151.4 0.9 copy.68
  152.3 0.0 copy-done.1
  (17 shorter events, 0.1 us)
Async XLA Ops:
  7.2 38.8 %copy-start = (f32[64,512]{1,0:T(8,128)S(1)}, f32[64,512]{1,0:T(8,128)}, u32[]{:S(2)}) copy-start(f32[64,512]{1,0:T(8,128)} %param.19) | copy-start | bytes 393220
  7.2 39.7 %copy-start.6 = (s32[512]{0:T(512)S(1)}, s32[512]{0:T(512)}, u32[]{:S(2)}) copy-start(s32[512]{0:T(512)} %param.21) | copy-start | bytes 6148
  7.2 40.1 %copy-start.5 = (f32[64,64]{1,0:T(8,128)S(1)}, f32[64,64]{1,0:T(8,128)}, u32[]{:S(2)}) copy-start(f32[64,64]{1,0:T(8,128)} %param.18) | copy-start | bytes 49156
  7.2 40.1 %copy-start.2 = (f32[2,1,512,64]{2,3,1,0:T(8,128)S(1)}, f32[2,1,512,64]{2,3,1,0:T(8,128)}, u32[]{:S(2)}) copy-start(f32[2,1,512,64]{2,3,1,0:T(8,128)} %param.13) | copy-start | bytes 786436
  7.2 41.7 %copy-start.3 = (f32[2,1,64,128]{3,2,1,0:T(8,128)S(1)}, f32[2,1,64,128]{3,2,1,0:T(8,128)}, u32[]{:S(2)}) copy-start(f32[2,1,64,128]{3,2,1,0:T(8,128)} %param.16) | copy-start | bytes 196612
  7.2 52.0 %copy-start.4 = (f32[2,1,64,128]{3,2,1,0:T(8,128)S(1)}, f32[2,1,64,128]{3,2,1,0:T(8,128)}, u32[]{:S(2)}) copy-start(f32[2,1,64,128]{3,2,1,0:T(8,128)} %param.17) | copy-start | bytes 196612
  7.2 98.6 %all-reduce.2.cloned.1.call-start = ((), (), s32[]{:S(2)}) async-start(), calls=%async_computation | async-start | bytes 524288 | tf_op jit(solution)/shard_map/psum | solution.py:72
  130.5 21.8 %copy-start.1 = (f32[2,64,512]{2,1,0:T(8,128)}, f32[2,64,512]{2,1,0:T(8,128)S(1)}, u32[]{:S(2)}) copy-start(f32[2,64,512]{2,1,0:T(8,128)S(1)} %fusion.12) | copy-start | bytes 786436
Sparse Core Ops, SparseCore 0:
  49.0 56.7 all-reduce.1
where the time goes:
time: 160 us; the launch traced here: 159 us
  blocking collectives  66.8 us (42%)
  other arithmetic  29.1 us (18%)
  waiting for transfers between devices  19.4 us (12%)
  local copies, waits for them, and re-layouts  15.2 us (10%)
  between operations  14.4 us (9%)
  matrix products  14.3 us (9%)
    psum x1, waiting for transfers between devices, body(): range_t = lax.psum(partial_range, 'col')  19.4 us
    all_gather x1, blocking collectives, body(): lax.all_gather(row_coeff, 'col', axis=3, tiled=True)  16.5 us
    all_gather x1, blocking collectives, body(): projected = lax.all_gather(projected_part, 'col', axis=2, tiled=True)  15.1 us
    all_gather x1, blocking collectives, body(): lax.all_gather(row_basis, 'col', axis=3, tiled=True)  14.8 us
    unnamed x19, local copies, waits for them, and re-layouts  12.3 us
    another operation x4, other arithmetic, body(): basis = tri_solve(jnp.linalg.cholesky(gram), range_t)  11.9 us
    all_gather x1, blocking collectives, body(): lax.all_gather(col_basis, 'row', axis=3, tiled=True)  10.3 us
    all_gather x1, blocking collectives, body(): lax.all_gather(col_scaled, 'row', axis=3, tiled=True)  10.2 us
  transfers between devices with their start and end apart: 1, of which 1 were waited for; matrix products, arithmetic and copies ran while one was open for 11% of the time, Pallas kernels for 0%

commit v1 on v0

--- a/solution.py
+++ b/solution.py
@@ -51,7 +51,7 @@
     )
     zcols, gcols = (
         lax.all_gather(col_basis, "row", axis=3, tiled=True),
-        lax.all_gather(col_scaled, "row", axis=3, tiled=True),
+        jnp.concatenate(lax.all_gather(col_scaled, "row"), axis=3),
     )
     xrows = xrows[:, 0]
     yrows = yrows[:, 0]

time: 160 us -> 160 us (level)
  no operation moved by 1% of the time
where the time goes in v1:
time: 160 us; the launch traced here: 159 us
  blocking collectives  66.1 us (41%)
  other arithmetic  29.1 us (18%)
  waiting for transfers between devices  19.8 us (12%)
  local copies, waits for them, and re-layouts  15.4 us (10%)
  between operations  14.4 us (9%)
  matrix products  14.2 us (9%)
    psum x1, waiting for transfers between devices, body(): range_t = lax.psum(partial_range, 'col')  19.8 us
    all_gather x1, blocking collectives, body(): lax.all_gather(row_coeff, 'col', axis=3, tiled=True)  16.5 us
    all_gather x1, blocking collectives, body(): projected = lax.all_gather(projected_part, 'col', axis=2, tiled=True)  15.1 us
    all_gather x1, blocking collectives, body(): lax.all_gather(row_basis, 'col', axis=3, tiled=True)  14.8 us
    unnamed x19, local copies, waits for them, and re-layouts  12.3 us
    another operation x4, other arithmetic, body(): basis = tri_solve(jnp.linalg.cholesky(gram), range_t)  11.9 us
    all_gather x1, blocking collectives, body(): lax.all_gather(col_basis, 'row', axis=3, tiled=True)  10.3 us
    another operation x3, other arithmetic, tri_solve(): jax.scipy.linalg.solve_triangular(low, right, lower=True)  9.92 us
  transfers between devices with their start and end apart: 1, of which 1 were waited for; matrix products, arithmetic and copies ran while one was open for 11% of the time, Pallas kernels for 0%

profile of v1, /device:TPU:0, one launch (start us, length us, event | category | flops | bytes accessed | tf_op | source)
XLA Modules:
  0.0 159.1 jit_solution(5318945160354107534)
XLA Ops:
  7.2 0.0 copy-start
  7.2 0.0 all-reduce.2.cloned.1.call-start
  7.3 0.8 broadcast_compare_fusion
  8.1 0.8 fusion.16
  8.9 0.9 copy.55
  9.8 0.9 copy.52
  10.8 1.0 copy.60
  11.8 16.5 %all_gather.18 = f32[2,1,64,512]{2,0,1,3:T(2,128)S(1)} all-gather(f32[2,1,64,64]{2,0,1,3:T(2,128)S(1)} %copy.52), channel_id=1, replica_groups=mesh['row'=4,'col'=8] {'col'}, dimensions={3}, use_global_device_ids=true | all-gather | bytes 294912 | tf_op jit(solution)/shard_map/all_gather | solution.py:50
  28.3 0.2 copy.53
  28.5 14.8 %all_gather.21 = f32[2,1,64,512]{2,0,1,3:T(2,128)S(1)} all-gather(f32[2,1,64,64]{2,0,1,3:T(2,128)S(1)} %copy.55), channel_id=1, replica_groups=mesh['row'=4,'col'=8] {'col'}, dimensions={3}, use_global_device_ids=true | all-gather | bytes 294912 | tf_op jit(solution)/shard_map/all_gather | solution.py:49
  43.3 0.2 copy.56
  43.5 2.2 %broadcast_select_fusion.4 = (f32[64,256,1]{0,2,1:T(1,128)S(1)}, f32[64,256,1]{0,2,1:T(1,128)S(1)}) fusion(pred[256]{0:T(512)(128)(4,1)S(1)} %broadcast_compare_fusion, f32[64,256,2]{0,2,1:T(2,128)S(1)} %bitcast.84, f32[256]{0:T(256)S(1)} %bitcast.93, f32[256]{0:T(256)S(1)} %bitcast.99, f32[256]{0:T(256)S(1)} %bitcast.96, f32[256]{0:T(256)S(1)} %bitcast.90), kind=kLoop, calls=%fused_computation.22 | loop fusion | flops 196608 | bytes 266496 | tf_op jit(solution)/shard_map/jit(_where)/select_n | solution.py:16
  45.7 0.3 pad_maximum_fusion
  46.0 0.5 fusion.6
  46.5 0.4 convolution_bitcast_fusion.2
  46.8 0.0 copy-done.6
  46.8 0.5 convolution_bitcast_fusion.3
  47.3 0.0 copy-done.5
  47.3 0.0 copy-done.2
  47.3 0.4 convolution_subtract_fusion
  47.7 1.1 convolution_bitcast_fusion.1
  48.8 0.0 all-reduce.2.cloned.1.call-update
  48.9 10.3 %all_gather.22 = f32[2,1,64,512]{3,2,0,1:T(8,128)S(1)} all-gather(f32[2,1,64,128]{3,2,0,1:T(8,128)S(1)} %bitcast.89), channel_id=1, replica_groups=mesh['row'=4,'col'=8] {'row'}, dimensions={3}, use_global_device_ids=true | all-gather | bytes 327680 | tf_op jit(solution)/shard_map/all_gather | solution.py:53
  59.2 9.5 %all-gather = f32[8,1,64,128]{3,2,1,0:T(8,128)S(1)} all-gather(f32[2,1,64,128]{3,2,1,0:T(8,128)S(1)} %copy-done.4), channel_id=2, replica_groups=mesh['row'=4,'col'=8] {'row'}, dimensions={0}, use_global_device_ids=true | all-gather | bytes 327680 | tf_op jit(solution)/shard_map/all_gather | solution.py:54
  68.7 0.2 copy.79
  68.9 0.1 reshape.149
  69.0 0.5 fusion.3
  69.5 0.6 convolution_bitcast_fusion
  70.1 7.2 %bitcast_subtract_fusion = f32[2,1,512,2,1,512]{5,2,0,3,4,1:T(8,128)} fusion(f32[2,1,512,2,1,512]{5,4,3,2,1,0:T(1,128)} %param.12, f32[2,512,2,64]{1,3,0,2:T(8,128)S(1)} %convolution_bitcast_fusion, f32[2,1,64,512]{3,2,0,1:T(8,128)S(1)} %all_gather.22), kind=kOutput, calls=%fused_computation.1 | convolution fusion | flops 806354944 | bytes 9175040 | tf_op jit(solution)/shard_map/apbs,bsq->apbq/dot_general | solution.py:62
  77.3 0.2 broadcast_in_dim.45
  77.5 8.5 %copy.67 = f32[2,1,512,2,1,512]{5,4,3,2,1,0:T(1,128)} copy(f32[2,1,512,2,1,512]{5,2,0,3,4,1:T(8,128)} %bitcast_subtract_fusion) | data formatting | bytes 8388608
  86.0 19.8 %all-reduce.2.cloned.1.call-done = f32[2,64,512]{2,1,0:T(8,128)} async-done(((f32[2,64,512]{2,1,0:T(8,128)}), f32[2,64,512]{2,1,0:T(8,128)}) %all-reduce.2.cloned.1.call-update) | async-done | bytes 262160 | tf_op jit(solution)/shard_map/psum | solution.py:72
  105.8 1.4 fusion.17
  107.2 0.1 copy.63
  107.3 11.7 %custom-call.8 = f32[2,64,64]{2,1,0:T(8,128)S(1)} custom-call(f32[2,64,64]{2,1,0:T(8,128)S(1)} %fusion.14), custom_call_target="Cholesky" | custom-call | tf_op jit(solution)/shard_map/jit(cholesky)/cholesky | solution.py:74
  119.1 0.1 compare_reduce_fusion
  119.2 0.1 select_bitcast_fusion
  119.3 9.8 %custom-call.9 = f32[2,1,64,64]{2,3,1,0:T(8,128)S(1)} custom-call(f32[2,1,64,64]{3,2,1,0:T(8,128)S(1)} %select_bitcast_fusion), custom_call_target="InvertDiagBlocksLowerTriangular" | custom-call | tf_op jit(solution)/shard_map/vmap(jit(_solve_triangular))/triangular_solve | solution.py:26
  129.1 1.4 fusion.12
  130.5 0.0 copy-start.1
  130.5 0.4 fusion.18
  130.9 0.1 copy.65
  131.0 15.1 %all_gather.23 = f32[2,64,512]{1,0,2:T(2,128)S(1)} all-gather(f32[2,64,64]{1,0,2:T(2,128)S(1)} %copy.65), channel_id=1, replica_groups=mesh['row'=4,'col'=8] {'col'}, dimensions={2}, use_global_device_ids=true | all-gather | bytes 294912 | tf_op jit(solution)/shard_map/all_gather | solution.py:76
  146.1 2.1 %gather_fusion = f32[512,2,64]{2,1,0:T(2,128)S(1)} fusion(f32[2,64,512]{1,0,2:T(2,128)S(1)} %all_gather.23, s32[1024]{0:T(1024)S(1)} %pad_clamp_fusion), kind=kCustom, calls=%fused_computation | custom fusion | bytes 526336 | tf_op jit(solution)/shard_map/jit(_take)/gather | solution.py:77
  148.2 0.4 broadcast_select_fusion.2
  148.6 2.2 %broadcast_select_fusion.1 = (f32[2,64,256,1]{1,3,2,0:T(1,128)S(1)}, f32[2,64,256,1]{1,3,2,0:T(1,128)S(1)}) fusion(pred[256]{0:T(512)(128)(4,1)S(1)} %broadcast_compare_fusion, f32[2,64,256,2]{1,3,2,0:T(2,128)S(1)} %broadcast_select_fusion.2, f32[256]{0:T(256)S(1)} %bitcast.95, f32[256]{0:T(256)S(1)} %multiply_subtract_fusion, f32[256]{0:T(256)S(1)} %bitcast.98, ...), kind=kLoop, calls=%fused_computation.9 | loop fusion | flops 393216 | bytes 528640 | tf_op jit(solution)/shard_map/jit(_where)/select_n | solution.py:16
  150.8 0.6 maximum_multiply_fusion
  151.4 0.9 copy.69
  (19 shorter events, 0.1 us)
Async XLA Ops:
  7.2 38.8 %copy-start = (f32[64,512]{1,0:T(8,128)S(1)}, f32[64,512]{1,0:T(8,128)}, u32[]{:S(2)}) copy-start(f32[64,512]{1,0:T(8,128)} %param.19) | copy-start | bytes 393220
  7.2 39.7 %copy-start.6 = (s32[512]{0:T(512)S(1)}, s32[512]{0:T(512)}, u32[]{:S(2)}) copy-start(s32[512]{0:T(512)} %param.21) | copy-start | bytes 6148
  7.2 40.1 %copy-start.5 = (f32[64,64]{1,0:T(8,128)S(1)}, f32[64,64]{1,0:T(8,128)}, u32[]{:S(2)}) copy-start(f32[64,64]{1,0:T(8,128)} %param.18) | copy-start | bytes 49156
  7.2 40.1 %copy-start.2 = (f32[2,1,512,64]{2,3,1,0:T(8,128)S(1)}, f32[2,1,512,64]{2,3,1,0:T(8,128)}, u32[]{:S(2)}) copy-start(f32[2,1,512,64]{2,3,1,0:T(8,128)} %param.13) | copy-start | bytes 786436
  7.2 41.7 %copy-start.3 = (f32[2,1,64,128]{3,2,1,0:T(8,128)S(1)}, f32[2,1,64,128]{3,2,1,0:T(8,128)}, u32[]{:S(2)}) copy-start(f32[2,1,64,128]{3,2,1,0:T(8,128)} %param.16) | copy-start | bytes 196612
  7.2 52.0 %copy-start.4 = (f32[2,1,64,128]{3,2,1,0:T(8,128)S(1)}, f32[2,1,64,128]{3,2,1,0:T(8,128)}, u32[]{:S(2)}) copy-start(f32[2,1,64,128]{3,2,1,0:T(8,128)} %param.17) | copy-start | bytes 196612
  7.2 98.6 %all-reduce.2.cloned.1.call-start = ((), (), s32[]{:S(2)}) async-start(), calls=%async_computation | async-start | bytes 524288 | tf_op jit(solution)/shard_map/psum | solution.py:72
  130.5 21.8 %copy-start.1 = (f32[2,64,512]{2,1,0:T(8,128)}, f32[2,64,512]{2,1,0:T(8,128)S(1)}, u32[]{:S(2)}) copy-start(f32[2,64,512]{2,1,0:T(8,128)S(1)} %fusion.12) | copy-start | bytes 786436
Sparse Core Ops, SparseCore 0:
  49.0 56.7 all-reduce.1
